TPU v7x, 32 devices: a whole 2x2x4 slice. The times are simulated.
32 devices in a mesh: seg: 8 (over z, y), blk: 4 (over x, core).
Axes of the slice: x: 2, y: 2, z: 4, core: 2. Of those that a mesh axis runs over, the one named last changes fastest.
Arguments:
- strain_rate: bfloat16 [2048, 16384], P('blk', 'seg'), may hold values from -1000 to 1000
- fir_taps: float32 [64], replicated, may hold values from -0.75 to 0.75
Outputs:
- correlation: float32 [2048, 2048, 128], P('blk', 'seg')
All inputs are finite; a program needn't handle non-finite values.
Results may differ from a plain program's by a relative error of at most 0.0023.
Values may be sent and summed in bfloat16 or wider, within the bound.
No kernel may reach another device: no remote copies, remote signals or barrier semaphores. Data moves between devices by JAX's collectives and lax.ppermute only.
A program may use at most 256 MiB of HBM per device.

v0:
```python
import math
import jax
import jax.numpy as jnp
from jax import lax
from jax.sharding import PartitionSpec as P

NFFT = 1024
NBIN = 128
FLO = 8
LAGS = 128
TAPS = 64
RAMW = 32
S_DEV = 2
epsilon = 1e-06


def with_halo(cells, sides, width):
    for axis, dim in sides:
        count = lax.axis_size(axis)
        ends = count - 1
        head = lax.slice_in_dim(cells, 0, width, axis=dim)
        tail = lax.slice_in_dim(cells, cells.shape[dim] - width, cells.shape[dim], axis=dim)
        cells = jnp.concatenate(
            [
                lax.ppermute(tail, axis, [(i, (i + 1) % count) for i in range(ends)]),
                cells,
                lax.ppermute(head, axis, [((i + 1) % count, i) for i in range(ends)]),
            ],
            axis=dim,
        )
    return cells


def broadcast(shard, axis, root):
    mine = lax.axis_index(axis) == root
    return lax.psum(jnp.where(mine, shard, jnp.zeros_like(shard)), axis)


def normalize(extended):
    window_len = 2 * RAMW + 1
    magnitude = jnp.abs(extended)
    running = lax.reduce_window(
        magnitude, jnp.zeros((), extended.dtype), lax.add, (1, window_len), (1, 1), "VALID"
    )
    return extended[:, RAMW : extended.shape[1] - RAMW] / (running / window_len + epsilon)


def band_matrix(fir_taps):
    rows_len = NFFT + TAPS
    padded = jnp.concatenate([fir_taps, jnp.zeros((rows_len + 2 - TAPS,), fir_taps.dtype)])
    tiled = jnp.tile(padded, NFFT // 2)[: NFFT // 2 * rows_len]
    return tiled.reshape(NFFT // 2, rows_len).T


def filter_blocks(normed, fir_taps):
    channels = normed.shape[0]
    groups = (normed.shape[1] - TAPS) // NFFT
    leading = normed[:, : groups * NFFT].reshape(channels, groups, NFFT)
    trailing = jnp.concatenate([leading[:, 1:, :TAPS], normed[:, None, groups * NFFT :]], axis=1)
    framed = jnp.concatenate([leading, trailing], axis=2)
    return jnp.einsum("cgw,wu->cgu", framed, band_matrix(fir_taps), precision=lax.Precision.HIGHEST)


def dft_table():
    sample_index = jnp.arange(NFFT, dtype=jnp.int32)[:, None]
    freq_index = jnp.arange(NBIN, dtype=jnp.int32)[None, :] + FLO
    phase_arg = (sample_index * freq_index % NFFT).astype(jnp.float32) * (2 * math.pi / NFFT)
    norm_scale = 1.0 / math.sqrt(NFFT)
    stacked = jnp.stack([jnp.cos(phase_arg) * norm_scale, -jnp.sin(phase_arg) * norm_scale], axis=2)
    return stacked.reshape(NFFT, 2 * NBIN)


def lag_table():
    freq_index = jnp.arange(NBIN, dtype=jnp.int32)[:, None] + FLO
    lag_index = jnp.arange(LAGS, dtype=jnp.int32)[None, :]
    phase_arg = (freq_index * lag_index % NFFT).astype(jnp.float32) * (2 * math.pi / NFFT)
    return jnp.cos(phase_arg)


def shards(strain_rate, fir_taps):
    channels, own_time = strain_rate.shape
    margin = RAMW + TAPS // 2
    reach_len = NFFT + margin
    widened = with_halo(strain_rate, (("seg", 1),), reach_len)
    extended = widened[:, reach_len - margin :].astype(jnp.float32)
    halves = filter_blocks(normalize(extended), fir_taps)
    dft_cols = dft_table()
    early_half = jnp.einsum(
        "csh,hk->ksc", halves[:, :-1], dft_cols[: NFFT // 2], precision=lax.Precision.HIGHEST
    )
    late_half = jnp.einsum(
        "csh,hk->ksc", halves[:, 1:], dft_cols[NFFT // 2 :], precision=lax.Precision.HIGHEST
    )
    spectra = (early_half + late_half).astype(jnp.bfloat16).reshape(NBIN, 2, S_DEV, channels)
    segs_total = S_DEV * lax.axis_size("seg")
    lag_cos = lag_table()
    gathered = lax.all_gather(spectra, "seg", axis=2, tiled=True)
    part_width = channels * lax.axis_size("blk") // lax.axis_size("seg")
    first_col = lax.axis_index("seg") * part_width
    source_block = broadcast(gathered, "blk", first_col // channels)
    partner = lax.dynamic_slice_in_dim(source_block, first_col % channels, part_width, 3)
    cross_spec = (
        jnp.einsum("fpsi,fpsj->fij", gathered, partner, preferred_element_type=jnp.float32)
        / segs_total
    )
    correlation = (
        jnp.einsum("fij,fl->ijl", cross_spec, lag_cos, precision=lax.Precision.HIGHEST) / NBIN
    )
    return correlation


def solution(mesh):
    return jax.shard_map(
        shards,
        mesh=mesh,
        in_specs=(P("blk", "seg"), P()),
        out_specs=P("blk", "seg", None),
        check_vma=False,
    )
```

profile of v0, /device:TPU:0, one launch (start us, length us, event | category | flops | bytes accessed | tf_op | source)
XLA Modules:
  0.0 578.1 jit_solution(5507240948475038173)
XLA Ops:
  6.5 2.9 copy.27
  10.9 5.1 collective-permute-start
  17.3 2.1 cosine_multiply_fusion
  20.4 2.0 copy.26
  22.4 2.2 reshape.133
  24.6 2.0 copy.31
  26.7 2.2 reshape.134
  30.5 4.5 tile.10
  34.9 3.1 slice.64
  38.1 3.4 reshape.130
  41.4 22.5 %collective-permute-done = bf16[512,1088]{0,1:T(8,128)(2,1)S(1)} collective-permute-done((bf16[512,1088]{0,1:T(8,128)(2,1)}, bf16[512,1088]{0,1:T(8,128)(2,1)S(1)}, u32[]{:S(2)}, u32[]{:S(2)}) %collective-permute-start) | collective-permute-done | bytes 1114144 | tf_op jit(solution)/shard_map/ppermute | solution.py:25
  63.9 5.0 fusion.56
  68.9 120.4 %reduce_window.7 = f32[512,3136]{0,1:T(8,128)} reduce-window(f32[512,3200]{0,1:T(8,128)} %fusion.56, f32[]{:T(128)} %constant.69.clone.1), window={size=1x65}, to_apply=%region_0.0 | reduce-window | flops 102760448 | bytes 12976132 | tf_op jit(solution)/shard_map/reduce_window | solution.py:42
  189.3 2.3 fusion.11
  192.5 4.4 slice_divide_fusion
  197.8 3.6 slice.61
  201.5 24.3 %fusion.4 = f32[512,3,512]{2,0,1:T(8,128)S(1)} fusion(f32[512,1,64]{0,2,1:T(8,128)S(1)} %slice_bitcast_fusion, f32[512,2,64]{0,2,1:T(8,128)S(1)} %slice.62, f32[512,3,1024]{0,2,1:T(8,128)S(1)} %bitcast.25, f32[512,1088]{1,0:T(8,128)S(1)} %copy-done.1), kind=kOutput, calls=%fused_computation.4 | convolution fusion | flops 10270998528 | bytes 12058624 | tf_op jit(solution)/shard_map/cgw,wu->cgu/dot_general | solution.py:61
  225.8 1.9 fusion.13
  227.8 1.9 fusion.24
  230.9 75.6 %all-gather.2.cloned.1.call-done = bf16[128,2,16,512]{3,0,1,2:T(8,128)(2,1)} async-done(((bf16[128,2,2,512]{3,0,1,2:T(8,128)(2,1)}), bf16[128,2,16,512]{3,0,1,2:T(8,128)(2,1)}) %all-gather.2.cloned.1.call-update) | async-done | bytes 4194320 | tf_op jit(solution)/shard_map/all_gather | solution.py:97
  306.5 6.6 %broadcast_select_fusion = bf16[128,2,16,512]{3,2,1,0:T(8,128)(2,1)} fusion(pred[]{:T(512)S(6)} %eq.9, bf16[128,2,16,512]{3,0,1,2:T(8,128)(2,1)} %all-gather.2.cloned.1.call-done), kind=kLoop, calls=%fused_computation.11 | loop fusion | flops 2097152 | bytes 8388609 | tf_op jit(solution)/shard_map/jit(_where)/select_n | solution.py:36
  313.2 83.9 %all-reduce.3.cloned.1.call-done = bf16[128,2,16,512]{3,2,1,0:T(8,128)(2,1)} async-done(((bf16[128,2,16,512]{3,2,1,0:T(8,128)(2,1)}), bf16[128,2,16,512]{3,2,1,0:T(8,128)(2,1)}) %all-reduce.3.cloned.1.call-update) | async-done | bytes 4194320 | tf_op jit(solution)/shard_map/psum | solution.py:36
  397.1 25.8 %bitcast_multiply_fusion = f32[128,512,256]{2,1,0:T(8,128)} fusion(bf16[128,2,16,512]{3,0,1,2:T(8,128)(2,1)} %all-gather.2.cloned.1.call-done, bf16[128,2,16,512]{3,2,1,0:T(8,128)(2,1)} %all-reduce.3.cloned.1.call-done, s32[]{:T(128)S(6)} %select_n.52), kind=kOutput, calls=%fused_computation | convolution fusion | flops 1090519040 | bytes 73400320 | tf_op jit(solution)/shard_map/fpsi,fpsj->fij/dot_general | solution.py:103
  422.9 148.2 %broadcast_multiply_fusion = f32[512,256,128]{2,1,0:T(8,128)} fusion(f32[128,512,256]{2,1,0:T(8,128)} %bitcast_multiply_fusion, s32[128]{0:T(128)S(1)} %iota_add_fusion), kind=kOutput, calls=%fused_computation.3 | convolution fusion | flops 25786810368 | bytes 134218240 | tf_op jit(solution)/shard_map/fij,fl->ijl/dot_general | solution.py:107
  (25 shorter events, 8.3 us)
Async XLA Ops:
  6.5 300.0 %all-gather.2.cloned.1.call-start = ((), (), s32[]{:S(2)}) async-start(), calls=%async_computation | async-start | bytes 4718592 | tf_op jit(solution)/shard_map/all_gather | solution.py:97
  10.9 18.0 %copy-start.4 = (f32[64]{0:T(128)S(1)}, f32[64]{0:T(128)}, u32[]{:S(2)}) copy-start(f32[64]{0:T(128)} %param.3) | copy-start | bytes 772
  10.9 53.0 %collective-permute-start = (bf16[512,1088]{0,1:T(8,128)(2,1)}, bf16[512,1088]{0,1:T(8,128)(2,1)S(1)}, u32[]{:S(2)}, u32[]{:S(2)}) collective-permute-start(bf16[512,1088]{0,1:T(8,128)(2,1)} %get-tuple-element.5), channel_id=1, source_target_pairs={{0,4},{4,8},{8,12},{12,16},{16,20},{20,24},{24,28},{1,5},{5,9},{9,... | collective-permute-start | bytes 3342344 | tf_op jit(solution)/shard_map/ppermute | solution.py:25
  16.0 47.9 %collective-permute-start.1 = (bf16[512,1088]{0,1:T(8,128)(2,1)}, bf16[512,1088]{0,1:T(8,128)(2,1)}, u32[]{:S(2)}, u32[]{:S(2)}) collective-permute-start(bf16[512,1088]{0,1:T(8,128)(2,1)} %get-tuple-element.6), channel_id=1, source_target_pairs={{4,0},{8,4},{12,8},{16,12},{20,16},{24,20},{28,24},{5,1},{9,5},{13... | collective-permute-start | bytes 3342344 | tf_op jit(solution)/shard_map/ppermute | solution.py:27
  189.3 3.2 copy-start
  197.8 3.7 copy-start.1
  201.5 24.4 %copy-start.2 = (f32[512,256,1]{0,1,2:T(8,128)S(1)}, f32[512,256,1]{0,1,2:T(8,128)}, u32[]{:S(2)}) copy-start(f32[512,256,1]{0,1,2:T(8,128)} %reshape.134) | copy-start | bytes 1572868
  201.5 26.3 %copy-start.3 = (f32[512,256,1]{0,1,2:T(8,128)S(1)}, f32[512,256,1]{0,1,2:T(8,128)}, u32[]{:S(2)}) copy-start(f32[512,256,1]{0,1,2:T(8,128)} %reshape.133) | copy-start | bytes 1572868
  230.8 166.3 %all-reduce.3.cloned.1.call-start = ((), (), s32[]{:S(2)}) async-start(), calls=%async_computation.1 | async-start | bytes 8388608 | tf_op jit(solution)/shard_map/psum | solution.py:36
Sparse Core Ops, SparseCore 0:
  231.0 75.5 all-gather.1
  313.3 83.7 all-reduce.2
where the time goes:
time: 584 us; the launch traced here: 578 us
  matrix products  202 us (35%)
  waiting for transfers between devices  182 us (31%)
  other arithmetic  142 us (24%)
  local copies, waits for them, and re-layouts  31.8 us (5%)
  between operations  13.8 us (2%)
  starting transfers between devices  6.4 us (1%)
    dot_general x1, matrix products, shards(): jnp.einsum('fij,fl->ijl', cross_spec, lag_cos, precision=lax.Precision.HI...  148 us
    another operation x1, other arithmetic, normalize(): lax.reduce_window(magnitude, jnp.zeros((), extended.dtype), lax.add, (1,...  120 us
    psum x1, waiting for transfers between devices, broadcast(): return lax.psum(jnp.where(mine, shard, jnp.zeros_like(shard)), axis)  83.9 us
    all_gather x1, waiting for transfers between devices, shards(): gathered = lax.all_gather(spectra, 'seg', axis=2, tiled=True)  75.6 us
    dot_general x1, matrix products, shards(): jnp.einsum('fpsi,fpsj->fij', gathered, partner, preferred_element_type=jn...  25.8 us
    dot_general x1, matrix products, filter_blocks(): jnp.einsum('cgw,wu->cgu', framed, band_matrix(fir_taps), precision=lax.Pr...  24.3 us
    ppermute x1, waiting for transfers between devices, with_halo(): lax.ppermute(tail, axis, [(i, (i + 1) % count) for i in range(ends)])  22.5 us
  transfers between devices with their start and end apart: 4, of which 3 were waited for; matrix products, arithmetic and copies ran while one was open for 4% of the time, Pallas kernels for 0%

commit v1 on v0

--- a/solution.py
+++ b/solution.py
@@ -12,6 +12,28 @@
 RAMW = 32
 S_DEV = 2
 epsilon = 1e-06
+
+
+def joined_along(blocks, dim):
+    shape = list(blocks.shape[1:])
+    shape[dim] *= blocks.shape[0]
+    return jnp.moveaxis(blocks, 0, dim).reshape(shape)
+
+
+def gather_around(shard, axis, dim):
+    peers = lax.axis_size(axis)
+    pairs = [(i, (i + 1) % peers) for i in range(peers)]
+    back = [(b, a) for a, b in pairs]
+    lower, upper = ([], [])
+    for step in range(peers - 1):
+        if step % 2 == 0:
+            lower.append(lax.ppermute(lower[-1] if lower else shard, axis, pairs))
+        else:
+            upper.append(lax.ppermute(upper[-1] if upper else shard, axis, back))
+    parts = jnp.stack([*lower[::-1], shard, *upper])
+    shift = lax.axis_index(axis) - len(lower)
+    parts = parts[(jnp.arange(peers) - shift) % peers]
+    return joined_along(parts, dim)
 
 
 def with_halo(cells, sides, width):
@@ -94,7 +116,7 @@
     spectra = (early_half + late_half).astype(jnp.bfloat16).reshape(NBIN, 2, S_DEV, channels)
     segs_total = S_DEV * lax.axis_size("seg")
     lag_cos = lag_table()
-    gathered = lax.all_gather(spectra, "seg", axis=2, tiled=True)
+    gathered = gather_around(spectra, "seg", 2)
     part_width = channels * lax.axis_size("blk") // lax.axis_size("seg")
     first_col = lax.axis_index("seg") * part_width
     source_block = broadcast(gathered, "blk", first_col // channels)

time: 584 us -> 621 us (1.063)
  local copies, waits for them, and re-layouts: 31.8 us -> 54.6 us
  starting transfers between devices: 6.4 us -> 21.2 us
    all_gather x1 -> x0, waiting for transfers between devices: 75.6 us -> none  [shards(): gathered = lax.all_gather(spectra, 'seg', axis=2, tiled=True)]
    ppermute x0 -> x7, waiting for transfers between devices: none -> 63.8 us  [the longest x4 52.1 us: gather_around(): lower.append(lax.ppermute(lower[-1] if lower else shard, axis, pairs))]
    ppermute x0 -> x7, starting transfers between devices: none -> 14.9 us  [the longest x3 9.95 us: gather_around(): upper.append(lax.ppermute(upper[-1] if upper else shard, axis, back))]
    gather x0 -> x1, local copies, waits for them, and re-layouts: none -> 12.1 us  [gather_around(): parts = parts[(jnp.arange(peers) - shift) % peers]]
    psum x1, waiting for transfers between devices: 83.9 us -> 94.3 us  [broadcast(): return lax.psum(jnp.where(mine, shard, jnp.zeros_like(shard)), axis)]
    unnamed x11 -> x18, local copies, waits for them, and re-layouts: 3.7 us -> 13.9 us
  transfers between devices with their start and end apart: 4 -> 10, of which waited for: 3 -> 9; matrix products, arithmetic and copies ran while one was open for 4% -> 6% of each run, Pallas kernels for 0% -> 0%
where the time goes in v1:
time: 621 us; the launch traced here: 614 us
  matrix products  202 us (33%)
  waiting for transfers between devices  181 us (29%)
  other arithmetic  142 us (23%)
  local copies, waits for them, and re-layouts  54.6 us (9%)
  starting transfers between devices  21.2 us (3%)
  between operations  14 us (2%)
    dot_general x1, matrix products, shards(): jnp.einsum('fij,fl->ijl', cross_spec, lag_cos, precision=lax.Precision.HI...  148 us
    another operation x1, other arithmetic, normalize(): lax.reduce_window(magnitude, jnp.zeros((), extended.dtype), lax.add, (1,...  120 us
    psum x1, waiting for transfers between devices, broadcast(): return lax.psum(jnp.where(mine, shard, jnp.zeros_like(shard)), axis)  94.3 us
    ppermute x4, waiting for transfers between devices, gather_around(): lower.append(lax.ppermute(lower[-1] if lower else shard, axis, pairs))  52.1 us
    dot_general x1, matrix products, shards(): jnp.einsum('fpsi,fpsj->fij', gathered, partner, preferred_element_type=jn...  25.8 us
    dot_general x1, matrix products, filter_blocks(): jnp.einsum('cgw,wu->cgu', framed, band_matrix(fir_taps), precision=lax.Pr...  24.2 us
    ppermute x1, waiting for transfers between devices, with_halo(): lax.ppermute(tail, axis, [(i, (i + 1) % count) for i in range(ends)])  22.5 us
    unnamed x18, local copies, waits for them, and re-layouts  13.9 us
  transfers between devices with their start and end apart: 10, of which 9 were waited for; matrix products, arithmetic and copies ran while one was open for 6% of the time, Pallas kernels for 0%

profile of v1, /device:TPU:0, one launch (start us, length us, event | category | flops | bytes accessed | tf_op | source)
XLA Modules:
  0.0 614.4 jit_solution(14814174991692401973)
XLA Ops:
  6.5 2.9 copy.17
  10.9 5.1 collective-permute-start
  30.5 4.5 tile.10
  35.0 3.1 slice.66
  38.1 3.4 reshape.182
  41.5 22.5 %collective-permute-done = bf16[512,1088]{0,1:T(8,128)(2,1)S(1)} collective-permute-done((bf16[512,1088]{0,1:T(8,128)(2,1)}, bf16[512,1088]{0,1:T(8,128)(2,1)S(1)}, u32[]{:S(2)}, u32[]{:S(2)}) %collective-permute-start) | collective-permute-done | bytes 1114144 | tf_op jit(solution)/shard_map/ppermute | solution.py:47
  63.9 5.0 fusion.58
  68.9 120.5 %reduce_window.7 = f32[512,3136]{0,1:T(8,128)} reduce-window(f32[512,3200]{0,1:T(8,128)} %fusion.58, f32[]{:T(128)} %constant.85.clone.1), window={size=1x65}, to_apply=%region_0.0 | reduce-window | flops 102760448 | bytes 12976132 | tf_op jit(solution)/shard_map/reduce_window | solution.py:64
  192.6 4.4 slice_divide_fusion
  197.8 3.6 slice.63
  201.6 24.2 %fusion.4 = f32[512,3,512]{2,0,1:T(8,128)S(1)} fusion(f32[512,1,64]{0,2,1:T(8,128)S(1)} %slice_bitcast_fusion, f32[512,2,64]{0,2,1:T(8,128)S(1)} %slice.64, f32[512,3,1024]{0,2,1:T(8,128)S(1)} %bitcast.48, f32[512,1088]{1,0:T(8,128)S(1)} %copy-done.1), kind=kOutput, calls=%fused_computation.5 | convolution fusion | flops 10270998528 | bytes 12058624 | tf_op jit(solution)/shard_map/cgw,wu->cgu/dot_general | solution.py:83
  232.4 14.2 %collective-permute-done.2 = bf16[128,2,2,512]{3,1,0,2:T(2,128)(2,1)S(1)} collective-permute-done((bf16[128,2,2,512]{3,1,0,2:T(2,128)(2,1)S(1)}, bf16[128,2,2,512]{3,1,0,2:T(2,128)(2,1)S(1)}, u32[]{:S(2)}, u32[]{:S(2)}) %collective-permute-start.2) | collective-permute-done | bytes 524320 | tf_op jit(solution)/shard_map/ppermute | solution.py:30
  246.5 4.7 collective-permute-start.6
  251.2 17.3 %collective-permute-done.3 = bf16[128,2,2,512]{3,1,0,2:T(2,128)(2,1)S(1)} collective-permute-done((bf16[128,2,2,512]{3,1,0,2:T(2,128)(2,1)S(1)}, bf16[128,2,2,512]{3,1,0,2:T(2,128)(2,1)S(1)}, u32[]{:S(2)}, u32[]{:S(2)}) %collective-permute-start.3) | collective-permute-done | bytes 524320 | tf_op jit(solution)/shard_map/ppermute | solution.py:30
  268.6 2.5 collective-permute-start.4
  274.1 10.8 %collective-permute-done.4 = bf16[128,2,2,512]{3,1,0,2:T(2,128)(2,1)} collective-permute-done((bf16[128,2,2,512]{3,1,0,2:T(2,128)(2,1)S(1)}, bf16[128,2,2,512]{3,1,0,2:T(2,128)(2,1)}, u32[]{:S(2)}, u32[]{:S(2)}) %collective-permute-start.4) | collective-permute-done | bytes 524320 | tf_op jit(solution)/shard_map/ppermute | solution.py:30
  285.2 10.0 %collective-permute-done.7 = bf16[128,2,2,512]{3,1,0,2:T(2,128)(2,1)S(1)} collective-permute-done((bf16[128,2,2,512]{3,1,0,2:T(2,128)(2,1)S(1)}, bf16[128,2,2,512]{3,1,0,2:T(2,128)(2,1)S(1)}, u32[]{:S(2)}, u32[]{:S(2)}) %collective-permute-start.7) | collective-permute-done | bytes 524320 | tf_op jit(solution)/shard_map/ppermute | solution.py:32
  295.2 2.9 collective-permute-start.8
  298.1 9.8 %collective-permute-done.5 = bf16[128,2,2,512]{3,1,0,2:T(2,128)(2,1)} collective-permute-done((bf16[128,2,2,512]{3,1,0,2:T(2,128)(2,1)}, bf16[128,2,2,512]{3,1,0,2:T(2,128)(2,1)}, u32[]{:S(2)}, u32[]{:S(2)}) %collective-permute-start.5) | collective-permute-done | bytes 524320 | tf_op jit(solution)/shard_map/ppermute | solution.py:30
  320.1 12.1 %gather_fusion = bf16[8,128,2,2,512]{4,2,1,3,0:T(2,128)(2,1)} fusion(bf16[8,128,2,2,512]{4,2,1,3,0:T(2,128)(2,1)} %bitcast_dynamic-update-slice_fusion, s32[1024]{0:T(1024)S(1)} %pad_clamp_fusion), kind=kCustom, calls=%fused_computation | custom fusion | bytes 8388640 | tf_op jit(solution)/shard_map/gather | solution.py:35
  332.2 6.6 %broadcast_select_fusion = bf16[128,2,16,512]{3,2,1,0:T(8,128)(2,1)} fusion(pred[]{:T(512)S(6)} %eq.11, bf16[128,2,16,512]{3,1,0,2:T(2,128)(2,1)} %bitcast.45), kind=kLoop, calls=%fused_computation.12 | loop fusion | flops 2097152 | bytes 8388609 | tf_op jit(solution)/shard_map/jit(_where)/select_n | solution.py:58
  338.9 94.3 %all-reduce.3.cloned.1.call-done = bf16[128,2,16,512]{3,2,1,0:T(8,128)(2,1)} async-done(((bf16[128,2,16,512]{3,2,1,0:T(8,128)(2,1)}), bf16[128,2,16,512]{3,2,1,0:T(8,128)(2,1)}) %all-reduce.3.cloned.1.call-update) | async-done | bytes 4194320 | tf_op jit(solution)/shard_map/psum | solution.py:58
  433.2 25.8 %bitcast_multiply_fusion = f32[128,512,256]{2,1,0:T(8,128)} fusion(bf16[128,2,16,512]{3,1,0,2:T(2,128)(2,1)} %bitcast.46, bf16[128,2,16,512]{3,2,1,0:T(8,128)(2,1)} %all-reduce.3.cloned.1.call-done, s32[]{:T(128)S(6)} %select_n.77), kind=kOutput, calls=%fused_computation.1 | convolution fusion | flops 1090519040 | bytes 73400320 | tf_op jit(solution)/shard_map/fpsi,fpsj->fij/dot_general | solution.py:125
  459.0 148.2 %broadcast_multiply_fusion = f32[512,256,128]{2,1,0:T(8,128)} fusion(f32[128,512,256]{2,1,0:T(8,128)} %bitcast_multiply_fusion, s32[128]{0:T(128)S(1)} %iota_add_fusion), kind=kOutput, calls=%fused_computation.4 | convolution fusion | flops 25786810368 | bytes 134218240 | tf_op jit(solution)/shard_map/fij,fl->ijl/dot_general | solution.py:129
  (47 shorter events, 42.1 us)
Async XLA Ops:
  6.5 426.7 %all-reduce.3.cloned.1.call-start = ((), (), s32[]{:S(2)}) async-start(), calls=%async_computation | async-start | bytes 8388608 | tf_op jit(solution)/shard_map/psum | solution.py:58
  10.9 18.0 %copy-start.4 = (f32[64]{0:T(128)S(1)}, f32[64]{0:T(128)}, u32[]{:S(2)}) copy-start(f32[64]{0:T(128)} %param.3) | copy-start | bytes 772
  10.9 53.0 %collective-permute-start = (bf16[512,1088]{0,1:T(8,128)(2,1)}, bf16[512,1088]{0,1:T(8,128)(2,1)S(1)}, u32[]{:S(2)}, u32[]{:S(2)}) collective-permute-start(bf16[512,1088]{0,1:T(8,128)(2,1)} %get-tuple-element.5), channel_id=1, source_target_pairs={{0,4},{4,8},{8,12},{12,16},{16,20},{20,24},{24,28},{1,5},{5,9},{9,... | collective-permute-start | bytes 3342344 | tf_op jit(solution)/shard_map/ppermute | solution.py:47
  16.0 47.9 %collective-permute-start.1 = (bf16[512,1088]{0,1:T(8,128)(2,1)}, bf16[512,1088]{0,1:T(8,128)(2,1)}, u32[]{:S(2)}, u32[]{:S(2)}) collective-permute-start(bf16[512,1088]{0,1:T(8,128)(2,1)} %get-tuple-element.6), channel_id=1, source_target_pairs={{4,0},{8,4},{12,8},{16,12},{20,16},{24,20},{28,24},{5,1},{9,5},{13... | collective-permute-start | bytes 3342344 | tf_op jit(solution)/shard_map/ppermute | solution.py:49
  189.4 3.2 copy-start
  197.8 3.7 copy-start.1
  201.5 24.3 %copy-start.2 = (f32[512,256,1]{0,1,2:T(8,128)S(1)}, f32[512,256,1]{0,1,2:T(8,128)}, u32[]{:S(2)}) copy-start(f32[512,256,1]{0,1,2:T(8,128)} %reshape.195) | copy-start | bytes 1572868
  201.5 26.2 %copy-start.3 = (f32[512,256,1]{0,1,2:T(8,128)S(1)}, f32[512,256,1]{0,1,2:T(8,128)}, u32[]{:S(2)}) copy-start(f32[512,256,1]{0,1,2:T(8,128)} %reshape.194) | copy-start | bytes 1572868
  229.9 16.6 %collective-permute-start.2 = (bf16[128,2,2,512]{3,1,0,2:T(2,128)(2,1)S(1)}, bf16[128,2,2,512]{3,1,0,2:T(2,128)(2,1)S(1)}, u32[]{:S(2)}, u32[]{:S(2)}) collective-permute-start(bf16[128,2,2,512]{3,1,0,2:T(2,128)(2,1)S(1)} %reshape.183), channel_id=1, source_target_pairs={{0,4},{4,8},{8,12},{12,16},{16,20},{20,24},{24,28},{28,0},{1,5},{5... | collective-permute-start | bytes 1572872 | tf_op jit(solution)/shard_map/ppermute | solution.py:30
  246.5 22.0 %collective-permute-start.3 = (bf16[128,2,2,512]{3,1,0,2:T(2,128)(2,1)S(1)}, bf16[128,2,2,512]{3,1,0,2:T(2,128)(2,1)S(1)}, u32[]{:S(2)}, u32[]{:S(2)}) collective-permute-start(bf16[128,2,2,512]{3,1,0,2:T(2,128)(2,1)S(1)} %collective-permute-done.2), channel_id=1, source_target_pairs={{0,4},{4,8},{8,12},{12,16},{16,20},{20,24},{24,28},{28,0},{1,5},{5... | collective-permute-start | bytes 1572872 | tf_op jit(solution)/shard_map/ppermute | solution.py:30
  246.5 25.3 %collective-permute-start.6 = (bf16[128,2,2,512]{3,1,0,2:T(2,128)(2,1)S(1)}, bf16[128,2,2,512]{3,1,0,2:T(2,128)(2,1)S(1)}, u32[]{:S(2)}, u32[]{:S(2)}) collective-permute-start(bf16[128,2,2,512]{3,1,0,2:T(2,128)(2,1)S(1)} %reshape.183), channel_id=1, source_target_pairs={{4,0},{8,4},{12,8},{16,12},{20,16},{24,20},{28,24},{0,28},{5,1},{9... | collective-permute-start | bytes 1572872 | tf_op jit(solution)/shard_map/ppermute | solution.py:32
  268.6 16.4 %collective-permute-start.4 = (bf16[128,2,2,512]{3,1,0,2:T(2,128)(2,1)S(1)}, bf16[128,2,2,512]{3,1,0,2:T(2,128)(2,1)}, u32[]{:S(2)}, u32[]{:S(2)}) collective-permute-start(bf16[128,2,2,512]{3,1,0,2:T(2,128)(2,1)S(1)} %collective-permute-done.3), channel_id=1, source_target_pairs={{0,4},{4,8},{8,12},{12,16},{16,20},{20,24},{24,28},{28,0},{1,5},{5... | collective-permute-start | bytes 1572872 | tf_op jit(solution)/shard_map/ppermute | solution.py:30
  271.8 23.4 %collective-permute-start.7 = (bf16[128,2,2,512]{3,1,0,2:T(2,128)(2,1)S(1)}, bf16[128,2,2,512]{3,1,0,2:T(2,128)(2,1)S(1)}, u32[]{:S(2)}, u32[]{:S(2)}) collective-permute-start(bf16[128,2,2,512]{3,1,0,2:T(2,128)(2,1)S(1)} %collective-permute-done.6), channel_id=1, source_target_pairs={{4,0},{8,4},{12,8},{16,12},{20,16},{24,20},{28,24},{0,28},{5,1},{9... | collective-permute-start | bytes 1572872 | tf_op jit(solution)/shard_map/ppermute | solution.py:32
  285.0 23.0 %collective-permute-start.5 = (bf16[128,2,2,512]{3,1,0,2:T(2,128)(2,1)}, bf16[128,2,2,512]{3,1,0,2:T(2,128)(2,1)}, u32[]{:S(2)}, u32[]{:S(2)}) collective-permute-start(bf16[128,2,2,512]{3,1,0,2:T(2,128)(2,1)} %collective-permute-done.4), channel_id=1, source_target_pairs={{0,4},{4,8},{8,12},{12,16},{16,20},{20,24},{24,28},{28,0},{1,5},{5... | collective-permute-start | bytes 1572872 | tf_op jit(solution)/shard_map/ppermute | solution.py:30
  295.2 23.8 %collective-permute-start.8 = (bf16[128,2,2,512]{3,1,0,2:T(2,128)(2,1)S(1)}, bf16[128,2,2,512]{3,1,0,2:T(2,128)(2,1)S(1)}, u32[]{:S(2)}, u32[]{:S(2)}) collective-permute-start(bf16[128,2,2,512]{3,1,0,2:T(2,128)(2,1)S(1)} %collective-permute-done.7), channel_id=1, source_target_pairs={{4,0},{8,4},{12,8},{16,12},{20,16},{24,20},{28,24},{0,28},{5,1},{9... | collective-permute-start | bytes 1572872 | tf_op jit(solution)/shard_map/ppermute | solution.py:32
Sparse Core Ops, SparseCore 0:
  339.0 94.1 all-reduce.2
